TPU v7x, 512 devices: a whole 4x4x16 slice. The times are simulated.
512 devices in a mesh: depth: 4 (over x), row: 8 (over y, core), col: 16 (over z).
Axes of the slice: x: 4, y: 4, z: 16, core: 2. Of those that a mesh axis runs over, the one named last changes fastest.
Arguments:
- species: float32 [2, 64, 256, 2048], P(None, 'depth', 'row', 'col'), may hold values from -6 to 6
- diffusivity: float32 [64, 256, 2048], P('depth', 'row', 'col'), may hold values from 0.05 to 0.4
- reaction_rate: float32 [64, 256, 2048], P('depth', 'row', 'col'), may hold values from 0.2 to 2
- shear_rate: float32 [16], replicated, may hold values from -0.08 to 0.08
- colour_weight: float32 [16, 4, 2], replicated, may hold values from -4 to 4
- colour_bias: float32 [16, 4], replicated, may hold values from -1 to 1
- slab_order: int32 [16, 4], replicated, may hold values from 0 to 3, each once within a row
- lengths: int32 [16, 16, 256], P('depth', 'col', 'row'), may hold values from 1 to 128
- owners: int32 [16, 16, 256, 1], P('depth', 'col', 'row'), may hold values from 0 to 15; in each aligned block of 32 rows (0 to 31, 32 to 63, ..., all dimensions but the last counted through in order) at most 4 rows name the same one
- warp_matrix: bfloat16 [16, 128, 128], replicated, may hold values from -0.5 to 0.5
Outputs:
- species_out: float32 [2, 64, 256, 2048], P(None, 'depth', 'row', 'col')
- frame: float32 [16, 256, 4, 2048], P('depth', 'row', None, 'col')
Inputs may be any that keep to these rules, and one draw needn't show every extreme that they name: `slab_order`: each row names each of the 4 slabs once. `owners`: for one view, the 32 scanlines of one device (aligned blocks of 32 along the third dimension) name any one owner at most 4 times.
All inputs are finite; a program needn't handle non-finite values.
Results may differ from a plain program's by a relative error of at most 0.001.
The roundings to bfloat16 on the way count: a program that leaves them out, or rounds other values in their place, can miss the bound.
Values may be sent and summed in bfloat16 or wider, within the bound.
No kernel may reach another device: no remote copies, remote signals or barrier semaphores. Data moves between devices by JAX's collectives and lax.ppermute only.
A program may use at most 64 MiB of HBM per device.

v0:
```python
import jax
import jax.numpy as jnp
from jax import lax
from jax.sharding import PartitionSpec as P

TIME_STEP = 0.1
RAY_STEP = 0.02
VEL_DEPTH = 0.3
VEL_ROW = 0.2
VEL_COL = 0.4


def with_halo(cells, sides, width):
    for axis, dim in sides:
        count = lax.axis_size(axis)
        ends = count - 1
        head = lax.slice_in_dim(cells, 0, width, axis=dim)
        tail = lax.slice_in_dim(cells, cells.shape[dim] - width, cells.shape[dim], axis=dim)
        cells = jnp.concatenate(
            [
                lax.ppermute(tail, axis, [(i, (i + 1) % count) for i in range(ends)]),
                cells,
                lax.ppermute(head, axis, [((i + 1) % count, i) for i in range(ends)]),
            ],
            axis=dim,
        )
    return cells


def tendency_of(padded, diffusivity, reaction_rate):
    centre = padded[:, 1:-1, 1:-1, 1:-1]
    below_depth = padded[:, :-2, 1:-1, 1:-1]
    above_depth = padded[:, 2:, 1:-1, 1:-1]
    below_row = padded[:, 1:-1, :-2, 1:-1]
    above_row = padded[:, 1:-1, 2:, 1:-1]
    below_col = padded[:, 1:-1, 1:-1, :-2]
    above_col = padded[:, 1:-1, 1:-1, 2:]
    laplace = (
        below_depth + above_depth + below_row + above_row + below_col + above_col - 6.0 * centre
    )
    advect = (
        VEL_DEPTH * (centre - below_depth)
        + VEL_ROW * (centre - below_row)
        + VEL_COL * (centre - below_col)
    )
    heat_part = centre[1]
    burned = reaction_rate * centre[0] * heat_part * heat_part / (1.0 + heat_part * heat_part)
    source = jnp.stack([-burned, burned])
    return diffusivity * laplace - advect + source


def with_faces(fields):
    return with_halo(fields.astype(jnp.bfloat16), (("depth", 1), ("row", 2), ("col", 3)), 1).astype(
        fields.dtype
    )


def advance(species, diffusivity, reaction_rate):
    first = species + TIME_STEP * tendency_of(with_faces(species), diffusivity, reaction_rate)
    second = 0.75 * species + 0.25 * (
        first + TIME_STEP * tendency_of(with_faces(first), diffusivity, reaction_rate)
    )
    return species / 3.0 + 2.0 / 3.0 * (
        second + TIME_STEP * tendency_of(with_faces(second), diffusivity, reaction_rate)
    )


def slot_plan(owner_rows, tiles):
    onehot = (owner_rows[..., None] == jnp.arange(tiles, dtype=jnp.int32)).astype(jnp.int32)
    running = jnp.cumsum(onehot, axis=-2)
    return jnp.sum(running * onehot, axis=-1) - 1


def body(
    species,
    diffusivity,
    reaction_rate,
    shear_rate,
    colour_weight,
    colour_bias,
    slab_order,
    lengths,
    owners,
    warp_matrix,
):
    depth_cells = species.shape[1]
    rows = species.shape[2]
    width = species.shape[3]
    depth_devices = lax.axis_size("depth")
    depth_total = depth_cells * depth_devices
    rim_width = (4 * depth_total + 99) // 100
    species_out = advance(species, diffusivity, reaction_rate)
    rimmed = with_halo(species_out, (("col", 3),), rim_width)
    slab_first = lax.axis_index("depth") * depth_cells
    views = shear_rate.shape[0]
    padded_width = width + 2 * rim_width
    rows_in = jnp.arange(padded_width, dtype=jnp.int32)[None, :, None]
    cols_out = jnp.arange(width, dtype=jnp.int32)[None, None, :]

    def march(state_pair, local_depth):
        colour, through = state_pair
        depth_index = slab_first + local_depth
        offset = shear_rate * (depth_index.astype(jnp.float32) + 0.5 - 0.5 * depth_total)
        floor_part = jnp.floor(offset)
        fraction = offset - floor_part
        start = floor_part.astype(jnp.int32) + rim_width
        target = cols_out + start[:, None, None]
        resample = jnp.where(rows_in == target, (1.0 - fraction)[:, None, None], 0.0) + jnp.where(
            rows_in == target + 1, fraction[:, None, None], 0.0
        )
        depth_plane = lax.dynamic_index_in_dim(rimmed, local_depth, 1, keepdims=False)
        samples = jnp.einsum(
            "fyp,vpx->vfyx", depth_plane, resample, precision=lax.Precision.HIGHEST
        )
        logits = (
            colour_weight[:, None, :, 0, None] * samples[:, 0][:, :, None, :]
            + colour_weight[:, None, :, 1, None] * samples[:, 1][:, :, None, :]
            + colour_bias[:, None, :, None]
        )
        colours = jax.nn.sigmoid(logits[:, :, :3, :])
        fading = jnp.exp(-RAY_STEP * jax.nn.softplus(logits[:, :, 3, :]))
        colour = colour + (through * (1.0 - fading))[:, :, None, :] * colours
        return ((colour, through * fading), None)

    start_state = (
        jnp.zeros((views, rows, 3, width), jnp.float32),
        jnp.ones((views, rows, width), jnp.float32),
    )
    (colour, through), unused = lax.scan(
        march, start_state, jnp.arange(depth_cells, dtype=jnp.int32)
    )
    slab = jnp.concatenate([colour, (1.0 - through)[:, :, None, :]], axis=2)
    view_count = views // depth_devices
    view_first = lax.axis_index("depth") * view_count
    everything = lax.all_gather(slab[None], "depth", axis=0, tiled=True)
    stack = lax.dynamic_slice_in_dim(everything, view_first, view_count, 1)
    own_order = lax.dynamic_slice_in_dim(slab_order, view_first, view_count, 0)
    slab_ids = jnp.arange(depth_devices, dtype=jnp.int32)

    def pick(position):
        chooser = (own_order[:, position][None, :] == slab_ids[:, None]).astype(jnp.float32)
        return jnp.sum(chooser[:, :, None, None, None] * stack, axis=0)

    result = pick(0)
    for position in range(1, depth_devices):
        result = result + (1.0 - result[:, :, 3:4, :]) * pick(position)
    picture = result.astype(jnp.bfloat16)
    column = jnp.arange(width, dtype=jnp.int32)
    keep = column[None, None, :] < lengths[:, 0, :, None]
    pieces = jnp.where(keep[:, :, None, :], picture, jnp.zeros((), jnp.bfloat16))
    tiles = lax.axis_size("col")
    capacity = 2 * rows // tiles
    mine = owners[:, 0, :, 0]
    slot_rank = slot_plan(mine, tiles)
    tile_ids = jnp.arange(tiles, dtype=jnp.int32)
    slot_ids = jnp.arange(capacity, dtype=jnp.int32)
    select = (mine[:, None, None, :] == tile_ids[None, :, None, None]) & (
        slot_rank[:, None, None, :] == slot_ids[None, None, :, None]
    )
    outgoing = jnp.einsum(
        "vosy,vycx->voscx", select.astype(jnp.bfloat16), pieces, preferred_element_type=jnp.float32
    ).astype(jnp.bfloat16)
    incoming = lax.all_to_all(outgoing, "col", split_axis=1, concat_axis=1, tiled=True)
    this_tile = lax.axis_index("col")
    owner_map = lax.all_gather(owners, "col", axis=1, tiled=True)[:, :, :, 0]
    source_rank = slot_plan(owner_map, tiles)
    place = (owner_map[:, :, None, :] == this_tile) & (
        source_rank[:, :, None, :] == slot_ids[None, None, :, None]
    )
    warp_own = lax.dynamic_slice_in_dim(warp_matrix, view_first, view_count, 0)
    warped = jnp.einsum("vtscx,vxz->vtscz", incoming, warp_own, preferred_element_type=jnp.float32)
    frame = jnp.einsum(
        "vtsy,vtscz->vycz", place.astype(jnp.float32), warped, precision=lax.Precision.HIGHEST
    )
    return (species_out, frame)


def solution(mesh):
    in_specs = (
        P(None, "depth", "row", "col"),
        P("depth", "row", "col"),
        P("depth", "row", "col"),
        P(),
        P(),
        P(),
        P(),
        P("depth", "col", "row"),
        P("depth", "col", "row", None),
        P(),
    )
    out_specs = (P(None, "depth", "row", "col"), P("depth", "row", None, "col"))
    return jax.shard_map(body, mesh=mesh, in_specs=in_specs, out_specs=out_specs, check_vma=False)
```

profile of v0, /device:TPU:8, one launch (start us, length us, event | category | flops | bytes accessed | tf_op | source)
XLA Modules:
  0.0 363.4 jit_solution(12064472902889304858)
XLA Ops:
  8.4 3.4 collective-permute-start
  13.2 4.2 %collective-permute-done.1 = bf16[2,1,32,128]{3,2,1,0:T(8,128)(2,1)S(1)} collective-permute-done((bf16[2,1,32,128]{3,2,1,0:T(8,128)(2,1)S(1)}, bf16[2,1,32,128]{3,2,1,0:T(8,128)(2,1)S(1)}, u32[]{:S(2)}, u32[]{:S(2)}) %collective-permute-start.1) | collective-permute-done | bytes 16416 | tf_op jit(solution)/shard_map/ppermute | solution.py:23
  19.4 3.6 %collective-permute-start.3 = (bf16[2,18,1,128]{3,2,1,0:T(2,128)(2,1)S(1)}, bf16[2,18,1,128]{3,2,1,0:T(2,128)(2,1)S(1)}, u32[]{:S(2)}, u32[]{:S(2)}) collective-permute-start(bf16[2,18,1,128]{3,2,1,0:T(2,128)(2,1)S(1)} %get-tuple-element.420), channel_id=1, source_target_pairs={{16,0},{32,16},{48,32},{64,48},{80,64},{96,80},{112,96},{17,1},{33... | collective-permute-start | bytes 27656 | tf_op jit(solution)/shard_map/ppermute | solution.py:23
  24.8 4.0 %collective-permute-start.4 = (bf16[2,18,34,1]{3,2,1,0:T(8,128)(2,1)S(1)}, bf16[2,18,34,1]{3,2,1,0:T(8,128)(2,1)S(1)}, u32[]{:S(2)}, u32[]{:S(2)}) collective-permute-start(bf16[2,18,34,1]{3,2,1,0:T(8,128)(2,1)S(1)} %get-tuple-element.413), channel_id=1, source_target_pairs={{0,1},{1,2},{2,3},{3,4},{4,5},{5,6},{6,7},{7,8},{8,9},{9,10},{10,1... | collective-permute-start | bytes 7352 | tf_op jit(solution)/shard_map/ppermute | solution.py:21
  30.3 6.8 %collective-permute-done.4 = bf16[2,18,34,1]{3,2,1,0:T(8,128)(2,1)S(1)} collective-permute-done((bf16[2,18,34,1]{3,2,1,0:T(8,128)(2,1)S(1)}, bf16[2,18,34,1]{3,2,1,0:T(8,128)(2,1)S(1)}, u32[]{:S(2)}, u32[]{:S(2)}) %collective-permute-start.4) | collective-permute-done | bytes 2480 | tf_op jit(solution)/shard_map/ppermute | solution.py:21
  37.1 4.7 %collective-permute-done.5 = bf16[2,18,34,1]{3,2,1,0:T(8,128)(2,1)S(1)} collective-permute-done((bf16[2,18,34,1]{3,2,1,0:T(8,128)(2,1)S(1)}, bf16[2,18,34,1]{3,2,1,0:T(8,128)(2,1)S(1)}, u32[]{:S(2)}, u32[]{:S(2)}) %collective-permute-start.5) | collective-permute-done | bytes 2480 | tf_op jit(solution)/shard_map/ppermute | solution.py:23
  43.5 3.4 collective-permute-start.6
  48.4 4.2 %collective-permute-done.7 = bf16[2,1,32,128]{3,2,1,0:T(8,128)(2,1)S(1)} collective-permute-done((bf16[2,1,32,128]{3,2,1,0:T(8,128)(2,1)S(1)}, bf16[2,1,32,128]{3,2,1,0:T(8,128)(2,1)S(1)}, u32[]{:S(2)}, u32[]{:S(2)}) %collective-permute-start.7) | collective-permute-done | bytes 16416 | tf_op jit(solution)/shard_map/ppermute | solution.py:23
  54.5 3.6 %collective-permute-start.9 = (bf16[2,18,1,128]{3,2,1,0:T(2,128)(2,1)S(1)}, bf16[2,18,1,128]{3,2,1,0:T(2,128)(2,1)S(1)}, u32[]{:S(2)}, u32[]{:S(2)}) collective-permute-start(bf16[2,18,1,128]{3,2,1,0:T(2,128)(2,1)S(1)} %get-tuple-element.418), channel_id=1, source_target_pairs={{16,0},{32,16},{48,32},{64,48},{80,64},{96,80},{112,96},{17,1},{33... | collective-permute-start | bytes 27656 | tf_op jit(solution)/shard_map/ppermute | solution.py:23
  60.0 3.8 %collective-permute-start.10 = (bf16[2,18,34,1]{3,2,1,0:T(8,128)(2,1)S(1)}, bf16[2,18,34,1]{3,2,1,0:T(8,128)(2,1)S(1)}, u32[]{:S(2)}, u32[]{:S(2)}) collective-permute-start(bf16[2,18,34,1]{3,2,1,0:T(8,128)(2,1)S(1)} %get-tuple-element.411), channel_id=1, source_target_pairs={{0,1},{1,2},{2,3},{3,4},{4,5},{5,6},{6,7},{7,8},{8,9},{9,10},{10,1... | collective-permute-start | bytes 7352 | tf_op jit(solution)/shard_map/ppermute | solution.py:21
  65.1 6.6 %collective-permute-done.10 = bf16[2,18,34,1]{3,2,1,0:T(8,128)(2,1)S(1)} collective-permute-done((bf16[2,18,34,1]{3,2,1,0:T(8,128)(2,1)S(1)}, bf16[2,18,34,1]{3,2,1,0:T(8,128)(2,1)S(1)}, u32[]{:S(2)}, u32[]{:S(2)}) %collective-permute-start.10) | collective-permute-done | bytes 2480 | tf_op jit(solution)/shard_map/ppermute | solution.py:21
  71.7 5.3 %collective-permute-done.11 = bf16[2,18,34,1]{3,2,1,0:T(8,128)(2,1)S(1)} collective-permute-done((bf16[2,18,34,1]{3,2,1,0:T(8,128)(2,1)S(1)}, bf16[2,18,34,1]{3,2,1,0:T(8,128)(2,1)S(1)}, u32[]{:S(2)}, u32[]{:S(2)}) %collective-permute-start.11) | collective-permute-done | bytes 2480 | tf_op jit(solution)/shard_map/ppermute | solution.py:23
  83.3 4.2 %collective-permute-done.13 = bf16[2,1,32,128]{3,2,1,0:T(8,128)(2,1)S(1)} collective-permute-done((bf16[2,1,32,128]{3,2,1,0:T(8,128)(2,1)S(1)}, bf16[2,1,32,128]{3,2,1,0:T(8,128)(2,1)S(1)}, u32[]{:S(2)}, u32[]{:S(2)}) %collective-permute-start.13) | collective-permute-done | bytes 16416 | tf_op jit(solution)/shard_map/ppermute | solution.py:23
  89.5 3.6 %collective-permute-start.15 = (bf16[2,18,1,128]{3,2,1,0:T(2,128)(2,1)S(1)}, bf16[2,18,1,128]{3,2,1,0:T(2,128)(2,1)S(1)}, u32[]{:S(2)}, u32[]{:S(2)}) collective-permute-start(bf16[2,18,1,128]{3,2,1,0:T(2,128)(2,1)S(1)} %get-tuple-element.416), channel_id=1, source_target_pairs={{16,0},{32,16},{48,32},{64,48},{80,64},{96,80},{112,96},{17,1},{33... | collective-permute-start | bytes 27656 | tf_op jit(solution)/shard_map/ppermute | solution.py:23
  95.0 5.4 %collective-permute-start.16 = (bf16[2,18,34,1]{3,2,1,0:T(8,128)(2,1)S(1)}, bf16[2,18,34,1]{3,2,1,0:T(8,128)(2,1)S(1)}, u32[]{:S(2)}, u32[]{:S(2)}) collective-permute-start(bf16[2,18,34,1]{3,2,1,0:T(8,128)(2,1)S(1)} %get-tuple-element.409), channel_id=1, source_target_pairs={{0,1},{1,2},{2,3},{3,4},{4,5},{5,6},{6,7},{7,8},{8,9},{9,10},{10,1... | collective-permute-start | bytes 7352 | tf_op jit(solution)/shard_map/ppermute | solution.py:21
  101.7 7.3 %collective-permute-done.16 = bf16[2,18,34,1]{3,2,1,0:T(8,128)(2,1)S(1)} collective-permute-done((bf16[2,18,34,1]{3,2,1,0:T(8,128)(2,1)S(1)}, bf16[2,18,34,1]{3,2,1,0:T(8,128)(2,1)S(1)}, u32[]{:S(2)}, u32[]{:S(2)}) %collective-permute-start.16) | collective-permute-done | bytes 2480 | tf_op jit(solution)/shard_map/ppermute | solution.py:21
  109.0 4.1 %collective-permute-done.17 = bf16[2,18,34,1]{3,2,1,0:T(8,128)(2,1)S(1)} collective-permute-done((bf16[2,18,34,1]{3,2,1,0:T(8,128)(2,1)S(1)}, bf16[2,18,34,1]{3,2,1,0:T(8,128)(2,1)S(1)}, u32[]{:S(2)}, u32[]{:S(2)}) %collective-permute-start.17) | collective-permute-done | bytes 2480 | tf_op jit(solution)/shard_map/ppermute | solution.py:23
  116.0 3.9 %collective-permute-start.18 = (f32[2,16,32,3]{3,2,1,0:T(8,128)}, f32[2,16,32,3]{3,2,1,0:T(8,128)S(1)}, u32[]{:S(2)}, u32[]{:S(2)}) collective-permute-start(f32[2,16,32,3]{3,2,1,0:T(8,128)} %get-tuple-element.407), channel_id=1, source_target_pairs={{0,1},{1,2},{2,3},{3,4},{4,5},{5,6},{6,7},{7,8},{8,9},{9,10},{10,1... | collective-permute-start | bytes 36872 | tf_op jit(solution)/shard_map/ppermute | solution.py:21
  121.5 9.1 %collective-permute-done.18 = f32[2,16,32,3]{3,2,1,0:T(8,128)S(1)} collective-permute-done((f32[2,16,32,3]{3,2,1,0:T(8,128)}, f32[2,16,32,3]{3,2,1,0:T(8,128)S(1)}, u32[]{:S(2)}, u32[]{:S(2)}) %collective-permute-start.18) | collective-permute-done | bytes 12320 | tf_op jit(solution)/shard_map/ppermute | solution.py:21
  131.3 3.8 %collective-permute-done.19 = f32[2,16,32,3]{3,2,1,0:T(8,128)} collective-permute-done((f32[2,16,32,3]{3,2,1,0:T(8,128)S(1)}, f32[2,16,32,3]{3,2,1,0:T(8,128)}, u32[]{:S(2)}, u32[]{:S(2)}) %collective-permute-start.19) | collective-permute-done | bytes 12320 | tf_op jit(solution)/shard_map/ppermute | solution.py:23
  136.9 108.8 %while.18 = (s32[]{:T(128)}, f32[16,32,3,128]{3,2,1,0:T(4,128)S(1)}, f32[16,32,128]{2,1,0:T(8,128)S(1)}, f32[16,4,2]{0,1,2:T(4,128)S(1)}, s32[16]{0:T(128)S(1)},...) while((s32[]{:T(128)}, ...), condition=%wide.region_5.6_spmd.clone.clone, body=%wide.region_4.5_spmd.clone.clone.sunk | while | flops 215089280 | bytes 12881818 | solution.py:129
  247.6 51.8 %all-gather.3.cloned.1.call-done = f32[64,32,4,128]{3,1,2,0:T(8,128)} async-done(((f32[16,32,4,128]{3,1,2,0:T(8,128)}), f32[64,32,4,128]{3,1,2,0:T(8,128)}) %all-gather.3.cloned.1.call-update) | async-done | bytes 4194320 | tf_op jit(solution)/shard_map/all_gather | solution.py:135
  302.4 12.3 %all-to-all-start = ((bf16[4,16,4,4,128]{4,3,2,0,1:T(4,128)(2,1)}), bf16[4,16,4,4,128]{4,3,2,0,1:T(4,128)(2,1)S(1)}, u32[]{:S(2)}, u32[]{:S(2)}) async-start(bf16[4,16,4,4,128]{4,3,2,0,1:T(4,128)(2,1)} %copy.51), calls=%async_computation | async-start | bytes 524288 | tf_op jit(solution)/shard_map/all_to_all | solution.py:163
  314.7 36.9 %all_gather.6 = s32[4,16,32,1]{2,3,1,0:T(1,128)S(1)} all-gather(s32[4,1,32,1]{2,3,1,0:T(1,128)S(1)} %copy-done.8), channel_id=1, replica_groups=mesh['depth'=4,'row'=8,'col'=16] {'col'}, dimensions={1}, use_global_device_ids=true | all-gather | bytes 8704 | tf_op jit(solution)/shard_map/all_gather | solution.py:165
  (362 shorter events, 107.7 us)
Async XLA Ops:
  7.2 347.8 %copy-start = (bf16[16,128,128]{2,1,0:T(8,128)(2,1)S(1)}, bf16[16,128,128]{2,1,0:T(8,128)(2,1)}, u32[]{:S(2)}) copy-start(bf16[16,128,128]{2,1,0:T(8,128)(2,1)} %param.21) | copy-start | bytes 1572868
  7.2 292.3 %all-gather.3.cloned.1.call-start = ((), (), s32[]{:S(2)}) async-start(), calls=%async_computation.1 | async-start | bytes 5242880 | tf_op jit(solution)/shard_map/all_gather | solution.py:135
  8.4 4.8 %collective-permute-start = (bf16[2,1,32,128]{3,2,1,0:T(8,128)(2,1)S(1)}, bf16[2,1,32,128]{3,2,1,0:T(8,128)(2,1)S(1)}, u32[]{:S(2)}, u32[]{:S(2)}) collective-permute-start(bf16[2,1,32,128]{3,2,1,0:T(8,128)(2,1)S(1)} %get-tuple-element.425), channel_id=1, source_target_pairs={{0,128},{128,256},{256,384},{1,129},{129,257},{257,385},{2,130},{1... | collective-permute-start | bytes 49160 | tf_op jit(solution)/shard_map/ppermute | solution.py:21
  11.8 5.6 %collective-permute-start.1 = (bf16[2,1,32,128]{3,2,1,0:T(8,128)(2,1)S(1)}, bf16[2,1,32,128]{3,2,1,0:T(8,128)(2,1)S(1)}, u32[]{:S(2)}, u32[]{:S(2)}) collective-permute-start(bf16[2,1,32,128]{3,2,1,0:T(8,128)(2,1)S(1)} %get-tuple-element.426), channel_id=1, source_target_pairs={{128,0},{256,128},{384,256},{129,1},{257,129},{385,257},{130,2},{2... | collective-permute-start | bytes 49160 | tf_op jit(solution)/shard_map/ppermute | solution.py:23
  17.4 5.6 %collective-permute-start.2 = (bf16[2,18,1,128]{3,2,1,0:T(2,128)(2,1)S(1)}, bf16[2,18,1,128]{3,2,1,0:T(2,128)(2,1)S(1)}, u32[]{:S(2)}, u32[]{:S(2)}) collective-permute-start(bf16[2,18,1,128]{3,2,1,0:T(2,128)(2,1)S(1)} %get-tuple-element.419), channel_id=1, source_target_pairs={{0,16},{16,32},{32,48},{48,64},{64,80},{80,96},{96,112},{1,17},{17... | collective-permute-start | bytes 27656 | tf_op jit(solution)/shard_map/ppermute | solution.py:21
  19.4 5.1 %collective-permute-start.3 = (bf16[2,18,1,128]{3,2,1,0:T(2,128)(2,1)S(1)}, bf16[2,18,1,128]{3,2,1,0:T(2,128)(2,1)S(1)}, u32[]{:S(2)}, u32[]{:S(2)}) collective-permute-start(bf16[2,18,1,128]{3,2,1,0:T(2,128)(2,1)S(1)} %get-tuple-element.420), channel_id=1, source_target_pairs={{16,0},{32,16},{48,32},{64,48},{80,64},{96,80},{112,96},{17,1},{33... | collective-permute-start | bytes 27656 | tf_op jit(solution)/shard_map/ppermute | solution.py:23
  24.8 12.2 %collective-permute-start.4 = (bf16[2,18,34,1]{3,2,1,0:T(8,128)(2,1)S(1)}, bf16[2,18,34,1]{3,2,1,0:T(8,128)(2,1)S(1)}, u32[]{:S(2)}, u32[]{:S(2)}) collective-permute-start(bf16[2,18,34,1]{3,2,1,0:T(8,128)(2,1)S(1)} %get-tuple-element.413), channel_id=1, source_target_pairs={{0,1},{1,2},{2,3},{3,4},{4,5},{5,6},{6,7},{7,8},{8,9},{9,10},{10,1... | collective-permute-start | bytes 7352 | tf_op jit(solution)/shard_map/ppermute | solution.py:21
  28.9 12.9 %collective-permute-start.5 = (bf16[2,18,34,1]{3,2,1,0:T(8,128)(2,1)S(1)}, bf16[2,18,34,1]{3,2,1,0:T(8,128)(2,1)S(1)}, u32[]{:S(2)}, u32[]{:S(2)}) collective-permute-start(bf16[2,18,34,1]{3,2,1,0:T(8,128)(2,1)S(1)} %get-tuple-element.414), channel_id=1, source_target_pairs={{1,0},{2,1},{3,2},{4,3},{5,4},{6,5},{7,6},{8,7},{9,8},{10,9},{11,1... | collective-permute-start | bytes 7352 | tf_op jit(solution)/shard_map/ppermute | solution.py:23
  43.5 4.8 %collective-permute-start.6 = (bf16[2,1,32,128]{3,2,1,0:T(8,128)(2,1)S(1)}, bf16[2,1,32,128]{3,2,1,0:T(8,128)(2,1)S(1)}, u32[]{:S(2)}, u32[]{:S(2)}) collective-permute-start(bf16[2,1,32,128]{3,2,1,0:T(8,128)(2,1)S(1)} %get-tuple-element.423), channel_id=1, source_target_pairs={{0,128},{128,256},{256,384},{1,129},{129,257},{257,385},{2,130},{1... | collective-permute-start | bytes 49160 | tf_op jit(solution)/shard_map/ppermute | solution.py:21
  46.9 5.6 %collective-permute-start.7 = (bf16[2,1,32,128]{3,2,1,0:T(8,128)(2,1)S(1)}, bf16[2,1,32,128]{3,2,1,0:T(8,128)(2,1)S(1)}, u32[]{:S(2)}, u32[]{:S(2)}) collective-permute-start(bf16[2,1,32,128]{3,2,1,0:T(8,128)(2,1)S(1)} %get-tuple-element.424), channel_id=1, source_target_pairs={{128,0},{256,128},{384,256},{129,1},{257,129},{385,257},{130,2},{2... | collective-permute-start | bytes 49160 | tf_op jit(solution)/shard_map/ppermute | solution.py:23
  52.6 5.6 %collective-permute-start.8 = (bf16[2,18,1,128]{3,2,1,0:T(2,128)(2,1)S(1)}, bf16[2,18,1,128]{3,2,1,0:T(2,128)(2,1)S(1)}, u32[]{:S(2)}, u32[]{:S(2)}) collective-permute-start(bf16[2,18,1,128]{3,2,1,0:T(2,128)(2,1)S(1)} %get-tuple-element.417), channel_id=1, source_target_pairs={{0,16},{16,32},{32,48},{48,64},{64,80},{80,96},{96,112},{1,17},{17... | collective-permute-start | bytes 27656 | tf_op jit(solution)/shard_map/ppermute | solution.py:21
  54.5 5.1 %collective-permute-start.9 = (bf16[2,18,1,128]{3,2,1,0:T(2,128)(2,1)S(1)}, bf16[2,18,1,128]{3,2,1,0:T(2,128)(2,1)S(1)}, u32[]{:S(2)}, u32[]{:S(2)}) collective-permute-start(bf16[2,18,1,128]{3,2,1,0:T(2,128)(2,1)S(1)} %get-tuple-element.418), channel_id=1, source_target_pairs={{16,0},{32,16},{48,32},{64,48},{80,64},{96,80},{112,96},{17,1},{33... | collective-permute-start | bytes 27656 | tf_op jit(solution)/shard_map/ppermute | solution.py:23
  60.0 11.8 %collective-permute-start.10 = (bf16[2,18,34,1]{3,2,1,0:T(8,128)(2,1)S(1)}, bf16[2,18,34,1]{3,2,1,0:T(8,128)(2,1)S(1)}, u32[]{:S(2)}, u32[]{:S(2)}) collective-permute-start(bf16[2,18,34,1]{3,2,1,0:T(8,128)(2,1)S(1)} %get-tuple-element.411), channel_id=1, source_target_pairs={{0,1},{1,2},{2,3},{3,4},{4,5},{5,6},{6,7},{7,8},{8,9},{9,10},{10,1... | collective-permute-start | bytes 7352 | tf_op jit(solution)/shard_map/ppermute | solution.py:21
  63.8 13.3 %collective-permute-start.11 = (bf16[2,18,34,1]{3,2,1,0:T(8,128)(2,1)S(1)}, bf16[2,18,34,1]{3,2,1,0:T(8,128)(2,1)S(1)}, u32[]{:S(2)}, u32[]{:S(2)}) collective-permute-start(bf16[2,18,34,1]{3,2,1,0:T(8,128)(2,1)S(1)} %get-tuple-element.412), channel_id=1, source_target_pairs={{1,0},{2,1},{3,2},{4,3},{5,4},{6,5},{7,6},{8,7},{9,8},{10,9},{11,1... | collective-permute-start | bytes 7352 | tf_op jit(solution)/shard_map/ppermute | solution.py:23
  78.8 4.5 %collective-permute-start.12 = (bf16[2,1,32,128]{3,2,1,0:T(8,128)(2,1)S(1)}, bf16[2,1,32,128]{3,2,1,0:T(8,128)(2,1)S(1)}, u32[]{:S(2)}, u32[]{:S(2)}) collective-permute-start(bf16[2,1,32,128]{3,2,1,0:T(8,128)(2,1)S(1)} %get-tuple-element.421), channel_id=1, source_target_pairs={{0,128},{128,256},{256,384},{1,129},{129,257},{257,385},{2,130},{1... | collective-permute-start | bytes 49160 | tf_op jit(solution)/shard_map/ppermute | solution.py:21
  81.9 5.6 %collective-permute-start.13 = (bf16[2,1,32,128]{3,2,1,0:T(8,128)(2,1)S(1)}, bf16[2,1,32,128]{3,2,1,0:T(8,128)(2,1)S(1)}, u32[]{:S(2)}, u32[]{:S(2)}) collective-permute-start(bf16[2,1,32,128]{3,2,1,0:T(8,128)(2,1)S(1)} %get-tuple-element.422), channel_id=1, source_target_pairs={{128,0},{256,128},{384,256},{129,1},{257,129},{385,257},{130,2},{2... | collective-permute-start | bytes 49160 | tf_op jit(solution)/shard_map/ppermute | solution.py:23
  87.6 5.6 %collective-permute-start.14 = (bf16[2,18,1,128]{3,2,1,0:T(2,128)(2,1)S(1)}, bf16[2,18,1,128]{3,2,1,0:T(2,128)(2,1)S(1)}, u32[]{:S(2)}, u32[]{:S(2)}) collective-permute-start(bf16[2,18,1,128]{3,2,1,0:T(2,128)(2,1)S(1)} %get-tuple-element.415), channel_id=1, source_target_pairs={{0,16},{16,32},{32,48},{48,64},{64,80},{80,96},{96,112},{1,17},{17... | collective-permute-start | bytes 27656 | tf_op jit(solution)/shard_map/ppermute | solution.py:21
  89.5 5.1 %collective-permute-start.15 = (bf16[2,18,1,128]{3,2,1,0:T(2,128)(2,1)S(1)}, bf16[2,18,1,128]{3,2,1,0:T(2,128)(2,1)S(1)}, u32[]{:S(2)}, u32[]{:S(2)}) collective-permute-start(bf16[2,18,1,128]{3,2,1,0:T(2,128)(2,1)S(1)} %get-tuple-element.416), channel_id=1, source_target_pairs={{16,0},{32,16},{48,32},{64,48},{80,64},{96,80},{112,96},{17,1},{33... | collective-permute-start | bytes 27656 | tf_op jit(solution)/shard_map/ppermute | solution.py:23
  95.0 14.1 %collective-permute-start.16 = (bf16[2,18,34,1]{3,2,1,0:T(8,128)(2,1)S(1)}, bf16[2,18,34,1]{3,2,1,0:T(8,128)(2,1)S(1)}, u32[]{:S(2)}, u32[]{:S(2)}) collective-permute-start(bf16[2,18,34,1]{3,2,1,0:T(8,128)(2,1)S(1)} %get-tuple-element.409), channel_id=1, source_target_pairs={{0,1},{1,2},{2,3},{3,4},{4,5},{5,6},{6,7},{7,8},{8,9},{9,10},{10,1... | collective-permute-start | bytes 7352 | tf_op jit(solution)/shard_map/ppermute | solution.py:21
  100.4 12.8 %collective-permute-start.17 = (bf16[2,18,34,1]{3,2,1,0:T(8,128)(2,1)S(1)}, bf16[2,18,34,1]{3,2,1,0:T(8,128)(2,1)S(1)}, u32[]{:S(2)}, u32[]{:S(2)}) collective-permute-start(bf16[2,18,34,1]{3,2,1,0:T(8,128)(2,1)S(1)} %get-tuple-element.410), channel_id=1, source_target_pairs={{1,0},{2,1},{3,2},{4,3},{5,4},{6,5},{7,6},{8,7},{9,8},{10,9},{11,1... | collective-permute-start | bytes 7352 | tf_op jit(solution)/shard_map/ppermute | solution.py:23
  114.9 22.0 %copy-start.1 = (f32[2,16,32,128]{3,2,1,0:T(8,128)}, f32[2,16,32,128]{3,2,1,0:T(8,128)S(1)}, u32[]{:S(2)}) copy-start(f32[2,16,32,128]{3,2,1,0:T(8,128)S(1)} %fusion.34) | copy-start | bytes 1572868
  116.0 14.6 %collective-permute-start.18 = (f32[2,16,32,3]{3,2,1,0:T(8,128)}, f32[2,16,32,3]{3,2,1,0:T(8,128)S(1)}, u32[]{:S(2)}, u32[]{:S(2)}) collective-permute-start(f32[2,16,32,3]{3,2,1,0:T(8,128)} %get-tuple-element.407), channel_id=1, source_target_pairs={{0,1},{1,2},{2,3},{3,4},{4,5},{5,6},{6,7},{7,8},{8,9},{9,10},{10,1... | collective-permute-start | bytes 36872 | tf_op jit(solution)/shard_map/ppermute | solution.py:21
  119.8 15.3 %collective-permute-start.19 = (f32[2,16,32,3]{3,2,1,0:T(8,128)S(1)}, f32[2,16,32,3]{3,2,1,0:T(8,128)}, u32[]{:S(2)}, u32[]{:S(2)}) collective-permute-start(f32[2,16,32,3]{3,2,1,0:T(8,128)S(1)} %get-tuple-element.408), channel_id=1, source_target_pairs={{1,0},{2,1},{3,2},{4,3},{5,4},{6,5},{7,6},{8,7},{9,8},{10,9},{11,1... | collective-permute-start | bytes 36872 | tf_op jit(solution)/shard_map/ppermute | solution.py:23
  302.4 52.6 %all-to-all-start = ((bf16[4,16,4,4,128]{4,3,2,0,1:T(4,128)(2,1)}), bf16[4,16,4,4,128]{4,3,2,0,1:T(4,128)(2,1)S(1)}, u32[]{:S(2)}, u32[]{:S(2)}) async-start(bf16[4,16,4,4,128]{4,3,2,0,1:T(4,128)(2,1)} %copy.51), calls=%async_computation | async-start | bytes 524288 | tf_op jit(solution)/shard_map/all_to_all | solution.py:163
  (42 other events, 179.4 us)
Sparse Core Ops, SparseCore 0:
  247.1 52.3 all-gather.2
where the time goes:
time: 365 us; the launch traced here: 363 us
  waiting for transfers between devices  117 us (32%)
  starting transfers between devices  65.4 us (18%)
  loops' own time  44.6 us (12%)
  local copies, waits for them, and re-layouts  37.4 us (10%)
  blocking collectives  36.9 us (10%)
  other arithmetic  28 us (8%)
  matrix products  19.4 us (5%)
  between operations  14.7 us (4%)
    all_gather x1, waiting for transfers between devices, body(): everything = lax.all_gather(slab[None], 'depth', axis=0, tiled=True)  51.8 us
    another operation x1, loops' own time, body(): lax.scan(march, start_state, jnp.arange(depth_cells, dtype=jnp.int32))  44.6 us
    all_gather x1, blocking collectives, body(): owner_map = lax.all_gather(owners, 'col', axis=1, tiled=True)[:, :, :, 0]  36.9 us
    ppermute x10, waiting for transfers between devices, with_halo(): lax.ppermute(head, axis, [((i + 1) % count, i) for i in range(ends)])  34.9 us
    ppermute x10, starting transfers between devices, with_halo(): lax.ppermute(tail, axis, [(i, (i + 1) % count) for i in range(ends)])  32.7 us
    ppermute x10, waiting for transfers between devices, with_halo(): lax.ppermute(tail, axis, [(i, (i + 1) % count) for i in range(ends)])  30.2 us
    while x96, local copies, waits for them, and re-layouts  20.6 us
    ppermute x10, starting transfers between devices, with_halo(): lax.ppermute(head, axis, [((i + 1) % count, i) for i in range(ends)])  20.3 us
  transfers between devices with their start and end apart: 22, of which 18 were waited for; matrix products, arithmetic and copies ran while one was open for 1% of the time, Pallas kernels for 0%

commit v1 on v0

--- a/solution.py
+++ b/solution.py
@@ -8,6 +8,11 @@
 VEL_DEPTH = 0.3
 VEL_ROW = 0.2
 VEL_COL = 0.4
+
+
+def gather_by_exchange(x, axis, dim):
+    copies = jnp.concatenate([x] * lax.axis_size(axis), axis=dim)
+    return lax.all_to_all(copies, axis, dim, dim, tiled=True)
 
 
 def with_halo(cells, sides, width):
@@ -162,7 +167,7 @@
     ).astype(jnp.bfloat16)
     incoming = lax.all_to_all(outgoing, "col", split_axis=1, concat_axis=1, tiled=True)
     this_tile = lax.axis_index("col")
-    owner_map = lax.all_gather(owners, "col", axis=1, tiled=True)[:, :, :, 0]
+    owner_map = gather_by_exchange(owners, "col", 1)[:, :, :, 0]
     source_rank = slot_plan(owner_map, tiles)
     place = (owner_map[:, :, None, :] == this_tile) & (
         source_rank[:, :, None, :] == slot_ids[None, None, :, None]

time: 365 us -> 344 us (0.942)
  blocking collectives: 36.9 us -> 0 us
  starting transfers between devices: 65.4 us -> 76.7 us
    all_gather x1 -> x0, blocking collectives: 36.9 us -> none  [body(): owner_map = lax.all_gather(owners, 'col', axis=1, tiled=True)[:, :, :, 0]]
    all_to_all x1, waiting for transfers between devices: 0.01 us -> 13.8 us  [body(): lax.all_to_all(outgoing, 'col', split_axis=1, concat_axis=1, tiled=True)]
    all_gather x1, waiting for transfers between devices: 51.8 us -> 39.6 us  [body(): everything = lax.all_gather(slab[None], 'depth', axis=0, tiled=True)]
    all_to_all x0 -> x1, starting transfers between devices: none -> 11.5 us  [gather_by_exchange(): return lax.all_to_all(copies, axis, dim, dim, tiled=True)]
  transfers between devices with their start and end apart: 22 -> 23, of which waited for: 18 -> 19; matrix products, arithmetic and copies ran while one was open for 1% -> 3% of each run, Pallas kernels for 0% -> 0%
where the time goes in v1:
time: 344 us; the launch traced here: 342 us
  waiting for transfers between devices  119 us (35%)
  starting transfers between devices  76.7 us (22%)
  loops' own time  44.8 us (13%)
  local copies, waits for them, and re-layouts  38.6 us (11%)
  other arithmetic  28.6 us (8%)
  matrix products  19.4 us (6%)
  between operations  14.7 us (4%)
    another operation x1, loops' own time, body(): lax.scan(march, start_state, jnp.arange(depth_cells, dtype=jnp.int32))  44.8 us
    all_gather x1, waiting for transfers between devices, body(): everything = lax.all_gather(slab[None], 'depth', axis=0, tiled=True)  39.6 us
    ppermute x10, waiting for transfers between devices, with_halo(): lax.ppermute(head, axis, [((i + 1) % count, i) for i in range(ends)])  34.9 us
    ppermute x10, starting transfers between devices, with_halo(): lax.ppermute(tail, axis, [(i, (i + 1) % count) for i in range(ends)])  32.7 us
    ppermute x10, waiting for transfers between devices, with_halo(): lax.ppermute(tail, axis, [(i, (i + 1) % count) for i in range(ends)])  30.4 us
    while x96, local copies, waits for them, and re-layouts  20.6 us
    ppermute x10, starting transfers between devices, with_halo(): lax.ppermute(head, axis, [((i + 1) % count, i) for i in range(ends)])  20.1 us
    dot_general x16, matrix products, march(): jnp.einsum('fyp,vpx->vfyx', depth_plane, resample, precision=lax.Precisio...  18.5 us
  transfers between devices with their start and end apart: 23, of which 19 were waited for; matrix products, arithmetic and copies ran while one was open for 3% of the time, Pallas kernels for 0%

profile of v1, /device:TPU:8, one launch (start us, length us, event | category | flops | bytes accessed | tf_op | source)
XLA Modules:
  0.0 341.5 jit_solution(2548796725877738732)
XLA Ops:
  13.2 4.2 %collective-permute-done.1 = bf16[2,1,32,128]{3,2,1,0:T(8,128)(2,1)S(1)} collective-permute-done((bf16[2,1,32,128]{3,2,1,0:T(8,128)(2,1)S(1)}, bf16[2,1,32,128]{3,2,1,0:T(8,128)(2,1)S(1)}, u32[]{:S(2)}, u32[]{:S(2)}) %collective-permute-start.1) | collective-permute-done | bytes 16416 | tf_op jit(solution)/shard_map/ppermute | solution.py:28
  19.4 3.6 %collective-permute-start.3 = (bf16[2,18,1,128]{3,2,1,0:T(2,128)(2,1)S(1)}, bf16[2,18,1,128]{3,2,1,0:T(2,128)(2,1)S(1)}, u32[]{:S(2)}, u32[]{:S(2)}) collective-permute-start(bf16[2,18,1,128]{3,2,1,0:T(2,128)(2,1)S(1)} %get-tuple-element.420), channel_id=1, source_target_pairs={{16,0},{32,16},{48,32},{64,48},{80,64},{96,80},{112,96},{17,1},{33... | collective-permute-start | bytes 27656 | tf_op jit(solution)/shard_map/ppermute | solution.py:28
  24.8 4.0 %collective-permute-start.4 = (bf16[2,18,34,1]{3,2,1,0:T(8,128)(2,1)S(1)}, bf16[2,18,34,1]{3,2,1,0:T(8,128)(2,1)S(1)}, u32[]{:S(2)}, u32[]{:S(2)}) collective-permute-start(bf16[2,18,34,1]{3,2,1,0:T(8,128)(2,1)S(1)} %get-tuple-element.413), channel_id=1, source_target_pairs={{0,1},{1,2},{2,3},{3,4},{4,5},{5,6},{6,7},{7,8},{8,9},{9,10},{10,1... | collective-permute-start | bytes 7352 | tf_op jit(solution)/shard_map/ppermute | solution.py:26
  30.3 6.8 %collective-permute-done.4 = bf16[2,18,34,1]{3,2,1,0:T(8,128)(2,1)S(1)} collective-permute-done((bf16[2,18,34,1]{3,2,1,0:T(8,128)(2,1)S(1)}, bf16[2,18,34,1]{3,2,1,0:T(8,128)(2,1)S(1)}, u32[]{:S(2)}, u32[]{:S(2)}) %collective-permute-start.4) | collective-permute-done | bytes 2480 | tf_op jit(solution)/shard_map/ppermute | solution.py:26
  37.1 4.7 %collective-permute-done.5 = bf16[2,18,34,1]{3,2,1,0:T(8,128)(2,1)S(1)} collective-permute-done((bf16[2,18,34,1]{3,2,1,0:T(8,128)(2,1)S(1)}, bf16[2,18,34,1]{3,2,1,0:T(8,128)(2,1)S(1)}, u32[]{:S(2)}, u32[]{:S(2)}) %collective-permute-start.5) | collective-permute-done | bytes 2480 | tf_op jit(solution)/shard_map/ppermute | solution.py:28
  43.5 3.4 collective-permute-start.6
  48.4 4.2 %collective-permute-done.7 = bf16[2,1,32,128]{3,2,1,0:T(8,128)(2,1)S(1)} collective-permute-done((bf16[2,1,32,128]{3,2,1,0:T(8,128)(2,1)S(1)}, bf16[2,1,32,128]{3,2,1,0:T(8,128)(2,1)S(1)}, u32[]{:S(2)}, u32[]{:S(2)}) %collective-permute-start.7) | collective-permute-done | bytes 16416 | tf_op jit(solution)/shard_map/ppermute | solution.py:28
  54.5 3.6 %collective-permute-start.9 = (bf16[2,18,1,128]{3,2,1,0:T(2,128)(2,1)S(1)}, bf16[2,18,1,128]{3,2,1,0:T(2,128)(2,1)S(1)}, u32[]{:S(2)}, u32[]{:S(2)}) collective-permute-start(bf16[2,18,1,128]{3,2,1,0:T(2,128)(2,1)S(1)} %get-tuple-element.418), channel_id=1, source_target_pairs={{16,0},{32,16},{48,32},{64,48},{80,64},{96,80},{112,96},{17,1},{33... | collective-permute-start | bytes 27656 | tf_op jit(solution)/shard_map/ppermute | solution.py:28
  60.0 3.8 %collective-permute-start.10 = (bf16[2,18,34,1]{3,2,1,0:T(8,128)(2,1)S(1)}, bf16[2,18,34,1]{3,2,1,0:T(8,128)(2,1)S(1)}, u32[]{:S(2)}, u32[]{:S(2)}) collective-permute-start(bf16[2,18,34,1]{3,2,1,0:T(8,128)(2,1)S(1)} %get-tuple-element.411), channel_id=1, source_target_pairs={{0,1},{1,2},{2,3},{3,4},{4,5},{5,6},{6,7},{7,8},{8,9},{9,10},{10,1... | collective-permute-start | bytes 7352 | tf_op jit(solution)/shard_map/ppermute | solution.py:26
  65.1 6.6 %collective-permute-done.10 = bf16[2,18,34,1]{3,2,1,0:T(8,128)(2,1)S(1)} collective-permute-done((bf16[2,18,34,1]{3,2,1,0:T(8,128)(2,1)S(1)}, bf16[2,18,34,1]{3,2,1,0:T(8,128)(2,1)S(1)}, u32[]{:S(2)}, u32[]{:S(2)}) %collective-permute-start.10) | collective-permute-done | bytes 2480 | tf_op jit(solution)/shard_map/ppermute | solution.py:26
  71.7 5.3 %collective-permute-done.11 = bf16[2,18,34,1]{3,2,1,0:T(8,128)(2,1)S(1)} collective-permute-done((bf16[2,18,34,1]{3,2,1,0:T(8,128)(2,1)S(1)}, bf16[2,18,34,1]{3,2,1,0:T(8,128)(2,1)S(1)}, u32[]{:S(2)}, u32[]{:S(2)}) %collective-permute-start.11) | collective-permute-done | bytes 2480 | tf_op jit(solution)/shard_map/ppermute | solution.py:28
  83.3 4.2 %collective-permute-done.13 = bf16[2,1,32,128]{3,2,1,0:T(8,128)(2,1)S(1)} collective-permute-done((bf16[2,1,32,128]{3,2,1,0:T(8,128)(2,1)S(1)}, bf16[2,1,32,128]{3,2,1,0:T(8,128)(2,1)S(1)}, u32[]{:S(2)}, u32[]{:S(2)}) %collective-permute-start.13) | collective-permute-done | bytes 16416 | tf_op jit(solution)/shard_map/ppermute | solution.py:28
  89.5 3.6 %collective-permute-start.15 = (bf16[2,18,1,128]{3,2,1,0:T(2,128)(2,1)S(1)}, bf16[2,18,1,128]{3,2,1,0:T(2,128)(2,1)S(1)}, u32[]{:S(2)}, u32[]{:S(2)}) collective-permute-start(bf16[2,18,1,128]{3,2,1,0:T(2,128)(2,1)S(1)} %get-tuple-element.416), channel_id=1, source_target_pairs={{16,0},{32,16},{48,32},{64,48},{80,64},{96,80},{112,96},{17,1},{33... | collective-permute-start | bytes 27656 | tf_op jit(solution)/shard_map/ppermute | solution.py:28
  95.0 5.4 %collective-permute-start.16 = (bf16[2,18,34,1]{3,2,1,0:T(8,128)(2,1)S(1)}, bf16[2,18,34,1]{3,2,1,0:T(8,128)(2,1)S(1)}, u32[]{:S(2)}, u32[]{:S(2)}) collective-permute-start(bf16[2,18,34,1]{3,2,1,0:T(8,128)(2,1)S(1)} %get-tuple-element.409), channel_id=1, source_target_pairs={{0,1},{1,2},{2,3},{3,4},{4,5},{5,6},{6,7},{7,8},{8,9},{9,10},{10,1... | collective-permute-start | bytes 7352 | tf_op jit(solution)/shard_map/ppermute | solution.py:26
  101.7 7.3 %collective-permute-done.16 = bf16[2,18,34,1]{3,2,1,0:T(8,128)(2,1)S(1)} collective-permute-done((bf16[2,18,34,1]{3,2,1,0:T(8,128)(2,1)S(1)}, bf16[2,18,34,1]{3,2,1,0:T(8,128)(2,1)S(1)}, u32[]{:S(2)}, u32[]{:S(2)}) %collective-permute-start.16) | collective-permute-done | bytes 2480 | tf_op jit(solution)/shard_map/ppermute | solution.py:26
  109.0 4.1 %collective-permute-done.17 = bf16[2,18,34,1]{3,2,1,0:T(8,128)(2,1)S(1)} collective-permute-done((bf16[2,18,34,1]{3,2,1,0:T(8,128)(2,1)S(1)}, bf16[2,18,34,1]{3,2,1,0:T(8,128)(2,1)S(1)}, u32[]{:S(2)}, u32[]{:S(2)}) %collective-permute-start.17) | collective-permute-done | bytes 2480 | tf_op jit(solution)/shard_map/ppermute | solution.py:28
  116.0 3.9 %collective-permute-start.18 = (f32[2,16,32,3]{3,2,1,0:T(8,128)}, f32[2,16,32,3]{3,2,1,0:T(8,128)S(1)}, u32[]{:S(2)}, u32[]{:S(2)}) collective-permute-start(f32[2,16,32,3]{3,2,1,0:T(8,128)} %get-tuple-element.407), channel_id=1, source_target_pairs={{0,1},{1,2},{2,3},{3,4},{4,5},{5,6},{6,7},{7,8},{8,9},{9,10},{10,1... | collective-permute-start | bytes 36872 | tf_op jit(solution)/shard_map/ppermute | solution.py:26
  121.3 9.3 %collective-permute-done.18 = f32[2,16,32,3]{3,2,1,0:T(8,128)S(1)} collective-permute-done((f32[2,16,32,3]{3,2,1,0:T(8,128)}, f32[2,16,32,3]{3,2,1,0:T(8,128)S(1)}, u32[]{:S(2)}, u32[]{:S(2)}) %collective-permute-start.18) | collective-permute-done | bytes 12320 | tf_op jit(solution)/shard_map/ppermute | solution.py:26
  131.3 3.8 %collective-permute-done.19 = f32[2,16,32,3]{3,2,1,0:T(8,128)} collective-permute-done((f32[2,16,32,3]{3,2,1,0:T(8,128)S(1)}, f32[2,16,32,3]{3,2,1,0:T(8,128)}, u32[]{:S(2)}, u32[]{:S(2)}) %collective-permute-start.19) | collective-permute-done | bytes 12320 | tf_op jit(solution)/shard_map/ppermute | solution.py:28
  136.9 108.8 %while.18 = (s32[]{:T(128)}, f32[16,32,3,128]{3,2,1,0:T(4,128)S(1)}, f32[16,32,128]{2,1,0:T(8,128)S(1)}, f32[16,4,2]{0,1,2:T(4,128)S(1)}, s32[16]{0:T(128)S(1)},...) while((s32[]{:T(128)}, ...), condition=%wide.region_5.6_spmd.clone.clone, body=%wide.region_4.5_spmd.clone.clone.sunk | while | flops 215089280 | bytes 12881818 | solution.py:134
  247.7 11.5 %all-to-all-start = ((s32[16,1,128]{2,1,0:T(1,128)}), s32[16,1,128]{2,1,0:T(1,128)S(1)}, u32[]{:S(2)}, u32[]{:S(2)}) async-start(s32[16,1,128]{2,1,0:T(1,128)} %reshape.223), calls=%async_computation | async-start | bytes 16384 | tf_op jit(solution)/shard_map/all_to_all | solution.py:15
  259.8 39.6 %all-gather.3.cloned.1.call-done = f32[64,32,4,128]{3,1,2,0:T(8,128)} async-done(((f32[16,32,4,128]{3,1,2,0:T(8,128)}), f32[64,32,4,128]{3,1,2,0:T(8,128)}) %all-gather.3.cloned.1.call-update) | async-done | bytes 4194320 | tf_op jit(solution)/shard_map/all_gather | solution.py:140
  302.4 12.3 %all-to-all-start.1 = ((bf16[4,16,4,4,128]{4,3,2,0,1:T(4,128)(2,1)}), bf16[4,16,4,4,128]{4,3,2,0,1:T(4,128)(2,1)S(1)}, u32[]{:S(2)}, u32[]{:S(2)}) async-start(bf16[4,16,4,4,128]{4,3,2,0,1:T(4,128)(2,1)} %copy.53), calls=%async_computation.1 | async-start | bytes 524288 | tf_op jit(solution)/shard_map/all_to_all | solution.py:168
  319.3 13.8 %all-to-all-done.1 = bf16[4,16,4,4,128]{4,3,2,0,1:T(4,128)(2,1)S(1)} async-done(((bf16[4,16,4,4,128]{4,3,2,0,1:T(4,128)(2,1)}), bf16[4,16,4,4,128]{4,3,2,0,1:T(4,128)(2,1)S(1)}, u32[]{:S(2)}, u32[]{:S(2)}) %all-to-all-start.1) | async-done | bytes 262176 | tf_op jit(solution)/shard_map/all_to_all | solution.py:168
  (370 shorter events, 112.8 us)
Async XLA Ops:
  7.2 326.0 %copy-start = (bf16[16,128,128]{2,1,0:T(8,128)(2,1)S(1)}, bf16[16,128,128]{2,1,0:T(8,128)(2,1)}, u32[]{:S(2)}) copy-start(bf16[16,128,128]{2,1,0:T(8,128)(2,1)} %param.21) | copy-start | bytes 1572868
  7.2 292.3 %all-gather.3.cloned.1.call-start = ((), (), s32[]{:S(2)}) async-start(), calls=%async_computation.2 | async-start | bytes 5242880 | tf_op jit(solution)/shard_map/all_gather | solution.py:140
  8.4 4.8 %collective-permute-start = (bf16[2,1,32,128]{3,2,1,0:T(8,128)(2,1)S(1)}, bf16[2,1,32,128]{3,2,1,0:T(8,128)(2,1)S(1)}, u32[]{:S(2)}, u32[]{:S(2)}) collective-permute-start(bf16[2,1,32,128]{3,2,1,0:T(8,128)(2,1)S(1)} %get-tuple-element.425), channel_id=1, source_target_pairs={{0,128},{128,256},{256,384},{1,129},{129,257},{257,385},{2,130},{1... | collective-permute-start | bytes 49160 | tf_op jit(solution)/shard_map/ppermute | solution.py:26
  11.8 5.6 %collective-permute-start.1 = (bf16[2,1,32,128]{3,2,1,0:T(8,128)(2,1)S(1)}, bf16[2,1,32,128]{3,2,1,0:T(8,128)(2,1)S(1)}, u32[]{:S(2)}, u32[]{:S(2)}) collective-permute-start(bf16[2,1,32,128]{3,2,1,0:T(8,128)(2,1)S(1)} %get-tuple-element.426), channel_id=1, source_target_pairs={{128,0},{256,128},{384,256},{129,1},{257,129},{385,257},{130,2},{2... | collective-permute-start | bytes 49160 | tf_op jit(solution)/shard_map/ppermute | solution.py:28
  17.4 5.6 %collective-permute-start.2 = (bf16[2,18,1,128]{3,2,1,0:T(2,128)(2,1)S(1)}, bf16[2,18,1,128]{3,2,1,0:T(2,128)(2,1)S(1)}, u32[]{:S(2)}, u32[]{:S(2)}) collective-permute-start(bf16[2,18,1,128]{3,2,1,0:T(2,128)(2,1)S(1)} %get-tuple-element.419), channel_id=1, source_target_pairs={{0,16},{16,32},{32,48},{48,64},{64,80},{80,96},{96,112},{1,17},{17... | collective-permute-start | bytes 27656 | tf_op jit(solution)/shard_map/ppermute | solution.py:26
  19.4 5.1 %collective-permute-start.3 = (bf16[2,18,1,128]{3,2,1,0:T(2,128)(2,1)S(1)}, bf16[2,18,1,128]{3,2,1,0:T(2,128)(2,1)S(1)}, u32[]{:S(2)}, u32[]{:S(2)}) collective-permute-start(bf16[2,18,1,128]{3,2,1,0:T(2,128)(2,1)S(1)} %get-tuple-element.420), channel_id=1, source_target_pairs={{16,0},{32,16},{48,32},{64,48},{80,64},{96,80},{112,96},{17,1},{33... | collective-permute-start | bytes 27656 | tf_op jit(solution)/shard_map/ppermute | solution.py:28
  24.8 12.2 %collective-permute-start.4 = (bf16[2,18,34,1]{3,2,1,0:T(8,128)(2,1)S(1)}, bf16[2,18,34,1]{3,2,1,0:T(8,128)(2,1)S(1)}, u32[]{:S(2)}, u32[]{:S(2)}) collective-permute-start(bf16[2,18,34,1]{3,2,1,0:T(8,128)(2,1)S(1)} %get-tuple-element.413), channel_id=1, source_target_pairs={{0,1},{1,2},{2,3},{3,4},{4,5},{5,6},{6,7},{7,8},{8,9},{9,10},{10,1... | collective-permute-start | bytes 7352 | tf_op jit(solution)/shard_map/ppermute | solution.py:26
  28.9 12.9 %collective-permute-start.5 = (bf16[2,18,34,1]{3,2,1,0:T(8,128)(2,1)S(1)}, bf16[2,18,34,1]{3,2,1,0:T(8,128)(2,1)S(1)}, u32[]{:S(2)}, u32[]{:S(2)}) collective-permute-start(bf16[2,18,34,1]{3,2,1,0:T(8,128)(2,1)S(1)} %get-tuple-element.414), channel_id=1, source_target_pairs={{1,0},{2,1},{3,2},{4,3},{5,4},{6,5},{7,6},{8,7},{9,8},{10,9},{11,1... | collective-permute-start | bytes 7352 | tf_op jit(solution)/shard_map/ppermute | solution.py:28
  43.5 4.8 %collective-permute-start.6 = (bf16[2,1,32,128]{3,2,1,0:T(8,128)(2,1)S(1)}, bf16[2,1,32,128]{3,2,1,0:T(8,128)(2,1)S(1)}, u32[]{:S(2)}, u32[]{:S(2)}) collective-permute-start(bf16[2,1,32,128]{3,2,1,0:T(8,128)(2,1)S(1)} %get-tuple-element.423), channel_id=1, source_target_pairs={{0,128},{128,256},{256,384},{1,129},{129,257},{257,385},{2,130},{1... | collective-permute-start | bytes 49160 | tf_op jit(solution)/shard_map/ppermute | solution.py:26
  46.9 5.6 %collective-permute-start.7 = (bf16[2,1,32,128]{3,2,1,0:T(8,128)(2,1)S(1)}, bf16[2,1,32,128]{3,2,1,0:T(8,128)(2,1)S(1)}, u32[]{:S(2)}, u32[]{:S(2)}) collective-permute-start(bf16[2,1,32,128]{3,2,1,0:T(8,128)(2,1)S(1)} %get-tuple-element.424), channel_id=1, source_target_pairs={{128,0},{256,128},{384,256},{129,1},{257,129},{385,257},{130,2},{2... | collective-permute-start | bytes 49160 | tf_op jit(solution)/shard_map/ppermute | solution.py:28
  52.6 5.6 %collective-permute-start.8 = (bf16[2,18,1,128]{3,2,1,0:T(2,128)(2,1)S(1)}, bf16[2,18,1,128]{3,2,1,0:T(2,128)(2,1)S(1)}, u32[]{:S(2)}, u32[]{:S(2)}) collective-permute-start(bf16[2,18,1,128]{3,2,1,0:T(2,128)(2,1)S(1)} %get-tuple-element.417), channel_id=1, source_target_pairs={{0,16},{16,32},{32,48},{48,64},{64,80},{80,96},{96,112},{1,17},{17... | collective-permute-start | bytes 27656 | tf_op jit(solution)/shard_map/ppermute | solution.py:26
  54.5 5.1 %collective-permute-start.9 = (bf16[2,18,1,128]{3,2,1,0:T(2,128)(2,1)S(1)}, bf16[2,18,1,128]{3,2,1,0:T(2,128)(2,1)S(1)}, u32[]{:S(2)}, u32[]{:S(2)}) collective-permute-start(bf16[2,18,1,128]{3,2,1,0:T(2,128)(2,1)S(1)} %get-tuple-element.418), channel_id=1, source_target_pairs={{16,0},{32,16},{48,32},{64,48},{80,64},{96,80},{112,96},{17,1},{33... | collective-permute-start | bytes 27656 | tf_op jit(solution)/shard_map/ppermute | solution.py:28
  60.0 11.8 %collective-permute-start.10 = (bf16[2,18,34,1]{3,2,1,0:T(8,128)(2,1)S(1)}, bf16[2,18,34,1]{3,2,1,0:T(8,128)(2,1)S(1)}, u32[]{:S(2)}, u32[]{:S(2)}) collective-permute-start(bf16[2,18,34,1]{3,2,1,0:T(8,128)(2,1)S(1)} %get-tuple-element.411), channel_id=1, source_target_pairs={{0,1},{1,2},{2,3},{3,4},{4,5},{5,6},{6,7},{7,8},{8,9},{9,10},{10,1... | collective-permute-start | bytes 7352 | tf_op jit(solution)/shard_map/ppermute | solution.py:26
  63.8 13.3 %collective-permute-start.11 = (bf16[2,18,34,1]{3,2,1,0:T(8,128)(2,1)S(1)}, bf16[2,18,34,1]{3,2,1,0:T(8,128)(2,1)S(1)}, u32[]{:S(2)}, u32[]{:S(2)}) collective-permute-start(bf16[2,18,34,1]{3,2,1,0:T(8,128)(2,1)S(1)} %get-tuple-element.412), channel_id=1, source_target_pairs={{1,0},{2,1},{3,2},{4,3},{5,4},{6,5},{7,6},{8,7},{9,8},{10,9},{11,1... | collective-permute-start | bytes 7352 | tf_op jit(solution)/shard_map/ppermute | solution.py:28
  78.8 4.5 %collective-permute-start.12 = (bf16[2,1,32,128]{3,2,1,0:T(8,128)(2,1)S(1)}, bf16[2,1,32,128]{3,2,1,0:T(8,128)(2,1)S(1)}, u32[]{:S(2)}, u32[]{:S(2)}) collective-permute-start(bf16[2,1,32,128]{3,2,1,0:T(8,128)(2,1)S(1)} %get-tuple-element.421), channel_id=1, source_target_pairs={{0,128},{128,256},{256,384},{1,129},{129,257},{257,385},{2,130},{1... | collective-permute-start | bytes 49160 | tf_op jit(solution)/shard_map/ppermute | solution.py:26
  81.9 5.6 %collective-permute-start.13 = (bf16[2,1,32,128]{3,2,1,0:T(8,128)(2,1)S(1)}, bf16[2,1,32,128]{3,2,1,0:T(8,128)(2,1)S(1)}, u32[]{:S(2)}, u32[]{:S(2)}) collective-permute-start(bf16[2,1,32,128]{3,2,1,0:T(8,128)(2,1)S(1)} %get-tuple-element.422), channel_id=1, source_target_pairs={{128,0},{256,128},{384,256},{129,1},{257,129},{385,257},{130,2},{2... | collective-permute-start | bytes 49160 | tf_op jit(solution)/shard_map/ppermute | solution.py:28
  87.6 5.6 %collective-permute-start.14 = (bf16[2,18,1,128]{3,2,1,0:T(2,128)(2,1)S(1)}, bf16[2,18,1,128]{3,2,1,0:T(2,128)(2,1)S(1)}, u32[]{:S(2)}, u32[]{:S(2)}) collective-permute-start(bf16[2,18,1,128]{3,2,1,0:T(2,128)(2,1)S(1)} %get-tuple-element.415), channel_id=1, source_target_pairs={{0,16},{16,32},{32,48},{48,64},{64,80},{80,96},{96,112},{1,17},{17... | collective-permute-start | bytes 27656 | tf_op jit(solution)/shard_map/ppermute | solution.py:26
  89.5 5.1 %collective-permute-start.15 = (bf16[2,18,1,128]{3,2,1,0:T(2,128)(2,1)S(1)}, bf16[2,18,1,128]{3,2,1,0:T(2,128)(2,1)S(1)}, u32[]{:S(2)}, u32[]{:S(2)}) collective-permute-start(bf16[2,18,1,128]{3,2,1,0:T(2,128)(2,1)S(1)} %get-tuple-element.416), channel_id=1, source_target_pairs={{16,0},{32,16},{48,32},{64,48},{80,64},{96,80},{112,96},{17,1},{33... | collective-permute-start | bytes 27656 | tf_op jit(solution)/shard_map/ppermute | solution.py:28
  95.0 14.1 %collective-permute-start.16 = (bf16[2,18,34,1]{3,2,1,0:T(8,128)(2,1)S(1)}, bf16[2,18,34,1]{3,2,1,0:T(8,128)(2,1)S(1)}, u32[]{:S(2)}, u32[]{:S(2)}) collective-permute-start(bf16[2,18,34,1]{3,2,1,0:T(8,128)(2,1)S(1)} %get-tuple-element.409), channel_id=1, source_target_pairs={{0,1},{1,2},{2,3},{3,4},{4,5},{5,6},{6,7},{7,8},{8,9},{9,10},{10,1... | collective-permute-start | bytes 7352 | tf_op jit(solution)/shard_map/ppermute | solution.py:26
  100.4 12.8 %collective-permute-start.17 = (bf16[2,18,34,1]{3,2,1,0:T(8,128)(2,1)S(1)}, bf16[2,18,34,1]{3,2,1,0:T(8,128)(2,1)S(1)}, u32[]{:S(2)}, u32[]{:S(2)}) collective-permute-start(bf16[2,18,34,1]{3,2,1,0:T(8,128)(2,1)S(1)} %get-tuple-element.410), channel_id=1, source_target_pairs={{1,0},{2,1},{3,2},{4,3},{5,4},{6,5},{7,6},{8,7},{9,8},{10,9},{11,1... | collective-permute-start | bytes 7352 | tf_op jit(solution)/shard_map/ppermute | solution.py:28
  116.0 14.6 %collective-permute-start.18 = (f32[2,16,32,3]{3,2,1,0:T(8,128)}, f32[2,16,32,3]{3,2,1,0:T(8,128)S(1)}, u32[]{:S(2)}, u32[]{:S(2)}) collective-permute-start(f32[2,16,32,3]{3,2,1,0:T(8,128)} %get-tuple-element.407), channel_id=1, source_target_pairs={{0,1},{1,2},{2,3},{3,4},{4,5},{5,6},{6,7},{7,8},{8,9},{9,10},{10,1... | collective-permute-start | bytes 36872 | tf_op jit(solution)/shard_map/ppermute | solution.py:26
  119.9 15.3 %collective-permute-start.19 = (f32[2,16,32,3]{3,2,1,0:T(8,128)S(1)}, f32[2,16,32,3]{3,2,1,0:T(8,128)}, u32[]{:S(2)}, u32[]{:S(2)}) collective-permute-start(f32[2,16,32,3]{3,2,1,0:T(8,128)S(1)} %get-tuple-element.408), channel_id=1, source_target_pairs={{1,0},{2,1},{3,2},{4,3},{5,4},{6,5},{7,6},{8,7},{9,8},{10,9},{11,1... | collective-permute-start | bytes 36872 | tf_op jit(solution)/shard_map/ppermute | solution.py:28
  247.7 54.7 %all-to-all-start = ((s32[16,1,128]{2,1,0:T(1,128)}), s32[16,1,128]{2,1,0:T(1,128)S(1)}, u32[]{:S(2)}, u32[]{:S(2)}) async-start(s32[16,1,128]{2,1,0:T(1,128)} %reshape.223), calls=%async_computation | async-start | bytes 16384 | tf_op jit(solution)/shard_map/all_to_all | solution.py:15
  302.4 30.7 %all-to-all-start.1 = ((bf16[4,16,4,4,128]{4,3,2,0,1:T(4,128)(2,1)}), bf16[4,16,4,4,128]{4,3,2,0,1:T(4,128)(2,1)S(1)}, u32[]{:S(2)}, u32[]{:S(2)}) async-start(bf16[4,16,4,4,128]{4,3,2,0,1:T(4,128)(2,1)} %copy.53), calls=%async_computation.1 | async-start | bytes 524288 | tf_op jit(solution)/shard_map/all_to_all | solution.py:168
  (43 other events, 225.4 us)
Sparse Core Ops, SparseCore 0:
  247.1 52.3 all-gather.2
